TPU v7x, 512 devices: a whole 4x8x8 slice. The times are simulated.
512 devices in a mesh: seq: 64 (over y, x, z_hi), tp: 8 (over z_lo, core).
Axes of the slice: x: 4, y: 8, z: 8 (z_hi: 2, z_lo: 4; z = z_hi * 4 + z_lo), core: 2. Of those that a mesh axis runs over, the one named last changes fastest.
Arguments:
- hidden_in: bfloat16 [16384, 2048], P('seq', 'tp'), may hold values from -6 to 6
- w_query: bfloat16 [2048, 2048], P(None, 'tp'), may hold values from -0.375 to 0.375
- w_keyval: bfloat16 [2048, 2, 2048], P(None, None, 'tp'), may hold values from -0.125 to 0.125
- w_out: bfloat16 [2048, 2048], P('tp'), may hold values from -0.125 to 0.125
- prompt_cache: bfloat16 [8192, 2, 2048], P('seq', None, 'tp'), may hold values from -160 to 160
- tail_cache: bfloat16 [128, 128, 2, 2048], P('seq', None, None, 'tp'), may hold values from -6 to 6
- tail_table: int32 [8, 16], replicated, may hold values from 0 to 127, as said below
- tail_len: int32 [8], replicated, may hold values from 1 to 2048
- shared_len: int32 [1], replicated, may hold values from 4096 to 8192
Outputs:
- hidden_out: bfloat16 [16384, 2048], P('seq', 'tp')
- new_cache: bfloat16 [16384, 2, 2048], P('seq', None, 'tp')
Inputs may be any that keep to these rules, and one draw needn't show every extreme that they name: Row r lists each of the slots r * 16 to (r + 1) * 16 - 1 once; block j of request r's tail is held in slot tail_table[r, j].
All inputs are finite; a program needn't handle non-finite values.
Results may differ from a plain program's by a relative error of at most 0.013.
Values may be sent and summed in bfloat16 or wider, within the bound.
A program may use at most 128 MiB of HBM per device.

v0:
```python
import jax
import jax.numpy as jnp
from jax import lax
from jax.sharding import PartitionSpec as P

HD = 128
REQ = 8
NEGATIVE = -1e30


def swapped(value, axis, stride):
    mask = 2**stride
    pairs = [(source, source ^ mask) for source in range(lax.axis_size(axis))]
    return lax.ppermute(value, axis, pairs)


def layer_norm(inputs):
    values = inputs.astype(jnp.float32)
    mean = jnp.mean(values, axis=-1, keepdims=True)
    centred = values - mean
    spread = jnp.mean(centred * centred, axis=-1, keepdims=True)
    return (centred * lax.rsqrt(spread + 1e-05)).astype(jnp.bfloat16)


def rotate(vectors, positions):
    half = vectors.shape[-1] // 2
    freqs = 10000.0 ** (-jnp.arange(half, dtype=jnp.float32) / half)
    angles = positions.astype(jnp.float32)[:, None, None] * freqs
    cosine = jnp.cos(angles)
    sine = jnp.sin(angles)
    first = vectors[..., :half]
    second = vectors[..., half:]
    return jnp.concatenate(
        [first * cosine - second * sine, second * cosine + first * sine], axis=-1
    )


def start_state(heads, queries, width):
    return (
        jnp.full((heads, queries), NEGATIVE, jnp.float32),
        jnp.zeros((heads, queries), jnp.float32),
        jnp.zeros((heads, queries, width), jnp.float32),
    )


def absorb(state, queries, keys, values, allowed):
    scores = jnp.einsum("hqd,khd->hqk", queries, keys, preferred_element_type=jnp.float32) * HD ** (
        -0.5
    )
    scores = jnp.where(allowed[None], scores, -jnp.inf)
    old_top, old_total, old_mixed = state
    new_top = jnp.maximum(old_top, jnp.max(scores, axis=2))
    factor = jnp.exp(old_top - new_top)
    weights = jnp.exp(scores - new_top[:, :, None])
    total = old_total * factor + jnp.sum(weights, axis=2)
    mixed = old_mixed * factor[:, :, None] + jnp.einsum(
        "hqk,khd->hqd", weights.astype(jnp.bfloat16), values, preferred_element_type=jnp.float32
    )
    return (new_top, total, mixed)


def combine(first, second):
    top = jnp.maximum(first[0], second[0])
    left = jnp.exp(first[0] - top)
    right = jnp.exp(second[0] - top)
    return (
        top,
        first[1] * left + second[1] * right,
        first[2] * left[:, :, None] + second[2] * right[:, :, None],
    )


def block_numbers(table_row, slot_ids):
    matches = table_row[None, :] == slot_ids[:, None]
    return jnp.sum(
        jnp.where(matches, jnp.arange(table_row.shape[0], dtype=jnp.int32)[None, :], 0), axis=1
    )


def local(
    hidden_in, w_query, w_keyval, w_out, prompt_cache, tail_cache, tail_table, tail_len, shared_len
):
    local_rows = hidden_in.shape[0]
    heads_here = w_query.shape[1] // HD
    group = lax.axis_size("seq") // REQ
    levels = group.bit_length() - 1
    seq_index = lax.axis_index("seq")
    request = seq_index // group
    member = seq_index % group
    offset = member * local_rows
    prompt_length = shared_len[0]
    own_length = lax.dynamic_index_in_dim(tail_len, request, 0, keepdims=False)
    table_row = lax.dynamic_index_in_dim(tail_table, request, 0, keepdims=False)
    slot_rows = tail_cache.shape[0]
    block_size = tail_cache.shape[1]
    whole = lax.all_gather(hidden_in, "tp", axis=1, tiled=True)
    normed = layer_norm(whole)
    query = jnp.dot(normed, w_query, preferred_element_type=jnp.float32).reshape(
        local_rows, heads_here, HD
    )
    projected = jnp.dot(
        normed, w_keyval.reshape(w_keyval.shape[0], -1), preferred_element_type=jnp.float32
    )
    projected = projected.reshape(local_rows, 2, heads_here, HD)
    positions = prompt_length + own_length + offset + jnp.arange(local_rows, dtype=jnp.int32)
    query = rotate(query, positions).astype(jnp.bfloat16)
    new_keys = rotate(projected[:, 0], positions).astype(jnp.bfloat16)
    new_values = projected[:, 1].astype(jnp.bfloat16)
    new_cache = jnp.stack(
        [new_keys.reshape(local_rows, -1), new_values.reshape(local_rows, -1)], axis=1
    )
    head_query = query.transpose(1, 0, 2)
    piece = lax.all_gather(prompt_cache, "seq", axis=0, tiled=True)
    length = piece.shape[0]
    allowed = (jnp.arange(length, dtype=jnp.int32) < prompt_length)[None, :]
    split = piece.reshape(length, 2, heads_here, HD)
    prompt_state = absorb(
        start_state(heads_here, local_rows, HD), head_query, split[:, 0], split[:, 1], allowed
    )
    packed = jnp.concatenate(
        [tail_cache.reshape(slot_rows * block_size, 2, tail_cache.shape[3]), new_cache], axis=0
    )
    per_member = packed.shape[0]
    for level in range(levels):
        other = swapped(packed, "seq", level)
        upper_half = seq_index // 2**level % 2 == 1
        packed = jnp.where(
            upper_half,
            jnp.concatenate([other, packed], axis=0),
            jnp.concatenate([packed, other], axis=0),
        )
    packed = packed.reshape(group, per_member, 2, heads_here, HD)
    tail_part = packed[:, : slot_rows * block_size].reshape(
        group * slot_rows * block_size, 2, heads_here, HD
    )
    fresh_part = packed[:, slot_rows * block_size :].reshape(group * local_rows, 2, heads_here, HD)
    slot_ids = request * group * slot_rows + jnp.arange(group * slot_rows, dtype=jnp.int32)
    tail_positions = (
        block_numbers(table_row, slot_ids)[:, None] * block_size
        + jnp.arange(block_size, dtype=jnp.int32)[None, :]
    ).reshape(-1)
    tail_allowed = (tail_positions < own_length)[None, :]
    fresh_allowed = (
        jnp.arange(group * local_rows, dtype=jnp.int32)[None, :]
        <= offset + jnp.arange(local_rows, dtype=jnp.int32)[:, None]
    )
    group_state = absorb(
        start_state(heads_here, local_rows, HD),
        head_query,
        tail_part[:, 0],
        tail_part[:, 1],
        tail_allowed,
    )
    group_state = absorb(group_state, head_query, fresh_part[:, 0], fresh_part[:, 1], fresh_allowed)
    final = combine(prompt_state, group_state)
    attended = (
        (final[2] / final[1][:, :, None])
        .astype(jnp.bfloat16)
        .transpose(1, 0, 2)
        .reshape(local_rows, -1)
    )
    summed = lax.psum_scatter(
        lax.dot_general(
            w_out, attended, (((0,), (1,)), ((), ())), preferred_element_type=jnp.float32
        ).astype(jnp.bfloat16),
        "tp",
        scatter_dimension=0,
        tiled=True,
    ).astype(jnp.float32)
    hidden_out = (hidden_in.astype(jnp.float32) + summed.T).astype(jnp.bfloat16)
    return (hidden_out, new_cache)


def solution(mesh):
    return jax.shard_map(
        local,
        mesh=mesh,
        in_specs=(
            P("seq", "tp"),
            P(None, "tp"),
            P(None, None, "tp"),
            P("tp", None),
            P("seq", None, "tp"),
            P("seq", None, None, "tp"),
            P(),
            P(),
            P(),
        ),
        out_specs=(P("seq", "tp"), P("seq", None, "tp")),
        check_vma=False,
    )
```

profile of v0, /device:TPU:12, one launch (start us, length us, event | category | flops | bytes accessed | tf_op | source)
XLA Modules:
  0.0 378.5 jit_solution(9868190781230296545)
XLA Ops:
  7.2 0.7 all-gather.3.cloned.1.call-update
  8.0 1.7 copy.36
  10.4 1.1 copy.50
  11.5 2.0 copy.57
  13.5 2.4 copy.39
  16.0 0.7 dynamic_slice.8
  17.4 0.5 multiply_cosine_fusion
  17.9 32.5 %all-gather.3.cloned.1.call-done = bf16[256,2048]{1,0:T(8,128)(2,1)} async-done(((bf16[256,256]{1,0:T(8,128)(2,1)}), bf16[256,2048]{1,0:T(8,128)(2,1)}) %all-gather.3.cloned.1.call-update) | async-done | bytes 1048592 | tf_op jit(solution)/shard_map/all_gather | solution.py:96
  50.4 1.6 convert_reduce_fusion
  52.0 1.6 fusion.16
  53.6 2.8 fusion.62
  56.5 0.7 fusion.85
  57.3 0.1 copy.51
  57.6 0.9 subtract_convert_fusion.1
  58.8 5.4 %collective-permute-start = (bf16[512,2,256]{0,2,1:T(8,128)(2,1)S(1)}, bf16[512,2,256]{0,2,1:T(8,128)(2,1)S(1)}, u32[]{:S(2)}, u32[]{:S(2)}) collective-permute-start(bf16[512,2,256]{0,2,1:T(8,128)(2,1)S(1)} %maximum_maximum_fusion), channel_id=1, source_target_pairs={{0,8},{8,0},{16,24},{24,16},{32,40},{40,32},{48,56},{56,48},{64,72... | collective-permute-start | bytes 1572872 | tf_op jit(solution)/shard_map/ppermute | solution.py:14
  64.2 25.7 %collective-permute-done = bf16[512,2,256]{0,2,1:T(8,128)(2,1)S(1)} collective-permute-done((bf16[512,2,256]{0,2,1:T(8,128)(2,1)S(1)}, bf16[512,2,256]{0,2,1:T(8,128)(2,1)S(1)}, u32[]{:S(2)}, u32[]{:S(2)}) %collective-permute-start) | collective-permute-done | bytes 524320 | tf_op jit(solution)/shard_map/ppermute | solution.py:14
  89.9 0.3 maximum_select_fusion.2
  90.2 3.1 collective-permute-start.1
  93.3 23.2 %collective-permute-done.1 = bf16[1024,2,256]{0,2,1:T(8,128)(2,1)} collective-permute-done((bf16[1024,2,256]{0,2,1:T(8,128)(2,1)S(1)}, bf16[1024,2,256]{0,2,1:T(8,128)(2,1)}, u32[]{:S(2)}, u32[]{:S(2)}) %collective-permute-start.1) | collective-permute-done | bytes 1048608 | tf_op jit(solution)/shard_map/ppermute | solution.py:14
  116.5 3.0 maximum_select_fusion.1
  119.5 2.7 collective-permute-start.2
  122.2 0.7 dynamic-slice_bitcast_fusion
  122.9 0.2 select_reduce_fusion
  123.1 0.8 fusion.65
  123.9 1.2 iota_compare_fusion
  125.1 43.9 %collective-permute-done.2 = bf16[2048,2,256]{0,2,1:T(8,128)(2,1)} collective-permute-done((bf16[2048,2,256]{0,2,1:T(8,128)(2,1)S(1)}, bf16[2048,2,256]{0,2,1:T(8,128)(2,1)}, u32[]{:S(2)}, u32[]{:S(2)}) %collective-permute-start.2) | collective-permute-done | bytes 2097184 | tf_op jit(solution)/shard_map/ppermute | solution.py:14
  169.0 3.7 maximum_select_fusion
  172.7 2.2 copy.58
  174.9 1.7 fusion.87
  176.6 4.6 %copy.56 = bf16[8,256,2,2,128]{4,1,0,3,2:T(8,128)(2,1)} copy(bf16[8,256,2,2,128]{1,0,4,3,2:T(8,128)(2,1)} %get-tuple-element.6) | data formatting | bytes 4194304
  181.2 2.9 copy.55
  184.1 2.2 fusion.7
  186.4 1.2 fusion.8
  187.6 0.7 copy-done.1
  188.3 1.3 copy-done.4
  189.6 2.0 fusion.9
  191.6 104.3 %all-gather.5.cloned.1.call-done = bf16[8192,2,256]{0,2,1:T(8,128)(2,1)} async-done(((bf16[128,2,256]{0,2,1:T(8,128)(2,1)}), bf16[8192,2,256]{0,2,1:T(8,128)(2,1)}) %all-gather.5.cloned.1.call-update) | async-done | bytes 8388624 | tf_op jit(solution)/shard_map/all_gather | solution.py:113
  295.9 9.6 %fusion = (f32[2,256]{1,0:T(2,128)S(1)}, f32[2,256,8192]{2,1,0:T(8,128)}) fusion(pred[8192]{0:T(1024)(128)(4,1)S(1)} %iota_compare_fusion.1, bf16[8192,2,2,128]{0,3,2,1:T(8,128)(2,1)} %bitcast.195, bf16[256,2,64]{2,0,1:T(8,128)(2,1)S(1)} %copy-done.14, bf16[256,2,64]{2,0,1:T(8,128)(2,1)S(1)} %copy-done.13), kind=kOutput, calls=%fused_computation.2 | convolution fusion | flops 1086586368 | bytes 21112832 | tf_op jit(solution)/shard_map/hqd,khd->hqk/dot_general | solution.py:47
  305.5 9.9 %fusion.1 = f32[2,256]{1,0:T(2,128)S(1)} fusion(f32[2,256,8192]{2,1,0:T(8,128)} %get-tuple-element.31, f32[2,256]{1,0:T(2,128)S(1)} %broadcast_maximum_fusion.1, pred[8192]{0:T(1024)(128)(4,1)S(1)} %iota_compare_fusion.1), kind=kLoop, calls=%fused_computation.3 | loop fusion | flops 16776704 | bytes 16789504 | tf_op jit(solution)/shard_map/reduce_sum | solution.py:55
  315.5 3.5 fusion.51
  319.1 0.5 copy-done.9
  319.6 1.3 fusion.45
  320.9 2.1 copy-done.10
  323.0 7.8 %fusion.57 = bf16[256,2,128]{0,2,1:T(8,128)(2,1)S(1)} fusion(f32[256,2,128]{0,2,1:T(8,128)S(1)} %fusion.45, bf16[8192,2,2,128]{0,3,2,1:T(8,128)(2,1)S(1)} %bitcast.196, f32[2,256,8192]{2,1,0:T(8,128)} %get-tuple-element.31, f32[2,256]{1,0:T(2,128)S(1)} %broadcast_maximum_fusion.1, pred[8192]{0:T(1024)(128)(4,1)S(1)} %iota_compare_fusion.1, ...), kind=kOutput, calls=%fused_computation.46 | convolution fusion | flops 1090846720 | bytes 21381120 | tf_op jit(solution)/shard_map/hqk,khd->hqd/dot_general | solution.py:56
  330.8 1.4 fusion.15
  332.3 0.9 copy.46
  333.2 37.2 %reduce-scatter.2.cloned.1.call-done = bf16[256,256]{0,1:T(8,128)(2,1)} async-done(((bf16[2048,256]{0,1:T(8,128)(2,1)}), bf16[256,256]{0,1:T(8,128)(2,1)}) %reduce-scatter.2.cloned.1.call-update) | async-done | bytes 131088 | tf_op jit(solution)/shard_map/reduce_scatter | solution.py:162
  370.4 1.6 fusion.64
  (57 shorter events, 0.9 us)
Async XLA Ops:
  7.2 323.7 %copy-start = (bf16[256,2048]{1,0:T(8,128)(2,1)S(1)}, bf16[256,2048]{1,0:T(8,128)(2,1)}, u32[]{:S(2)}) copy-start(bf16[256,2048]{1,0:T(8,128)(2,1)} %param.12) | copy-start | bytes 3145732
  7.2 43.2 %all-gather.3.cloned.1.call-start = ((), (), s32[]{:S(2)}) async-start(), calls=%async_computation.1 | async-start | bytes 1179648 | tf_op jit(solution)/shard_map/all_gather | solution.py:96
  7.9 288.0 %all-gather.5.cloned.1.call-start = ((), (), s32[]{:S(2)}) async-start(), calls=%async_computation.2 | async-start | bytes 8519680 | tf_op jit(solution)/shard_map/all_gather | solution.py:113
  9.7 360.7 %reduce-scatter.2.cloned.1.call-start = ((), (), s32[]{:S(2)}) async-start(), calls=%async_computation.3 | async-start | bytes 1179648 | tf_op jit(solution)/shard_map/reduce_scatter | solution.py:162
  11.5 4.5 %copy-start.17 = (s32[8]{0:T(128)S(1)}, s32[8]{0:T(128)}, u32[]{:S(2)}) copy-start(s32[8]{0:T(128)} %param.16) | copy-start | bytes 100
  50.4 6.1 %copy-start.6 = (bf16[256,2048]{1,0:T(8,128)(2,1)S(1)}, bf16[256,2048]{1,0:T(8,128)(2,1)}, u32[]{:S(2)}) copy-start(bf16[256,2048]{1,0:T(8,128)(2,1)} %all-gather.3.cloned.1.call-done) | copy-start | bytes 3145732
  50.4 6.1 %copy-start.16 = (bf16[2048,256]{1,0:T(8,128)(2,1)S(1)}, bf16[2048,256]{1,0:T(8,128)(2,1)}, u32[]{:S(2)}) copy-start(bf16[2048,256]{1,0:T(8,128)(2,1)} %param.10) | copy-start | bytes 3145732
  58.7 34.6 %copy-start.11 = (bf16[256,2,128]{0,2,1:T(8,128)(2,1)}, bf16[256,2,128]{0,2,1:T(8,128)(2,1)S(1)}, u32[]{:S(2)}) copy-start(bf16[256,2,128]{0,2,1:T(8,128)(2,1)S(1)} %copy.41) | copy-start | bytes 393220
  58.8 31.1 %collective-permute-start = (bf16[512,2,256]{0,2,1:T(8,128)(2,1)S(1)}, bf16[512,2,256]{0,2,1:T(8,128)(2,1)S(1)}, u32[]{:S(2)}, u32[]{:S(2)}) collective-permute-start(bf16[512,2,256]{0,2,1:T(8,128)(2,1)S(1)} %maximum_maximum_fusion), channel_id=1, source_target_pairs={{0,8},{8,0},{16,24},{24,16},{32,40},{40,32},{48,56},{56,48},{64,72... | collective-permute-start | bytes 1572872 | tf_op jit(solution)/shard_map/ppermute | solution.py:14
  90.2 3.1 copy-start.3
  90.2 26.3 %collective-permute-start.1 = (bf16[1024,2,256]{0,2,1:T(8,128)(2,1)S(1)}, bf16[1024,2,256]{0,2,1:T(8,128)(2,1)}, u32[]{:S(2)}, u32[]{:S(2)}) collective-permute-start(bf16[1024,2,256]{0,2,1:T(8,128)(2,1)S(1)} %maximum_select_fusion.2), channel_id=1, source_target_pairs={{0,16},{8,24},{16,0},{24,8},{32,48},{40,56},{48,32},{56,40},{64,80... | collective-permute-start | bytes 3145736 | tf_op jit(solution)/shard_map/ppermute | solution.py:14
  119.5 49.4 %collective-permute-start.2 = (bf16[2048,2,256]{0,2,1:T(8,128)(2,1)S(1)}, bf16[2048,2,256]{0,2,1:T(8,128)(2,1)}, u32[]{:S(2)}, u32[]{:S(2)}) collective-permute-start(bf16[2048,2,256]{0,2,1:T(8,128)(2,1)S(1)} %maximum_select_fusion.1), channel_id=1, source_target_pairs={{0,32},{8,40},{16,48},{24,56},{32,0},{40,8},{48,16},{56,24},{64,96... | collective-permute-start | bytes 6291464 | tf_op jit(solution)/shard_map/ppermute | solution.py:14
  176.6 7.5 %copy-start.13 = (bf16[256,2,64]{2,0,1:T(8,128)(2,1)S(1)}, bf16[256,2,64]{2,0,1:T(8,128)(2,1)}, u32[]{:S(2)}) copy-start(bf16[256,2,64]{2,0,1:T(8,128)(2,1)} %get-tuple-element.8) | copy-start | bytes 196612
  176.6 7.5 %copy-start.14 = (bf16[256,2,64]{2,0,1:T(8,128)(2,1)S(1)}, bf16[256,2,64]{2,0,1:T(8,128)(2,1)}, u32[]{:S(2)}) copy-start(bf16[256,2,64]{2,0,1:T(8,128)(2,1)} %get-tuple-element.9) | copy-start | bytes 196612
  184.1 2.2 copy-start.7
  184.1 2.2 copy-start.8
  186.4 2.0 copy-start.1
  187.6 2.0 copy-start.4
  305.5 10.0 %copy-start.2 = (bf16[8,256,2,2,128]{4,1,0,3,2:T(8,128)(2,1)S(1)}, bf16[8,256,2,2,128]{4,1,0,3,2:T(8,128)(2,1)}, u32[]{:S(2)}) copy-start(bf16[8,256,2,2,128]{4,1,0,3,2:T(8,128)(2,1)} %copy.55) | copy-start | bytes 6291460
  315.5 3.6 copy-start.5
  315.5 4.1 %copy-start.9 = (bf16[8,256,2,2,128]{4,1,0,3,2:T(8,128)(2,1)S(1)}, bf16[8,256,2,2,128]{4,1,0,3,2:T(8,128)(2,1)}, u32[]{:S(2)}) copy-start(bf16[8,256,2,2,128]{4,1,0,3,2:T(8,128)(2,1)} %copy.56) | copy-start | bytes 6291460
  319.6 3.4 copy-start.10
  323.0 9.3 %copy-start.12 = (bf16[256,2,128]{0,2,1:T(8,128)(2,1)S(1)}, bf16[256,2,128]{0,2,1:T(8,128)(2,1)}, u32[]{:S(2)}) copy-start(bf16[256,2,128]{0,2,1:T(8,128)(2,1)} %copy-done.11) | copy-start | bytes 393220
  330.8 39.6 %copy-start.15 = (bf16[256,256]{1,0:T(8,128)(2,1)S(1)}, bf16[256,256]{1,0:T(8,128)(2,1)}, u32[]{:S(2)}) copy-start(bf16[256,256]{1,0:T(8,128)(2,1)} %param.9) | copy-start | bytes 393220
Sparse Core Ops, SparseCore 0:
  10.0 40.3 all-gather.2
  54.7 241.2 all-gather.4
  332.4 37.9 reduce-scatter.1
where the time goes:
time: 379 us; the launch traced here: 378 us
  waiting for transfers between devices  267 us (70%)
  matrix products  30.5 us (8%)
  other arithmetic  27.6 us (7%)
  local copies, waits for them, and re-layouts  26.1 us (7%)
  between operations  15.6 us (4%)
  starting transfers between devices  11.3 us (3%)
    all_gather x1, waiting for transfers between devices, local(): piece = lax.all_gather(prompt_cache, 'seq', axis=0, tiled=True)  104 us
    ppermute x3, waiting for transfers between devices, swapped(): return lax.ppermute(value, axis, pairs)  92.8 us
    reduce_scatter x1, waiting for transfers between devices, local(): lax.psum_scatter(lax.dot_general(w_out, attended, (((0,), (1,)), ((), ())...  37.2 us
    all_gather x1, waiting for transfers between devices, local(): whole = lax.all_gather(hidden_in, 'tp', axis=1, tiled=True)  32.5 us
    unnamed x45, local copies, waits for them, and re-layouts  19.4 us
    dot_general x3, matrix products, absorb(): jnp.einsum('hqd,khd->hqk', queries, keys, preferred_element_type=jnp.floa...  13 us
    dot_general x3, matrix products, absorb(): jnp.einsum('hqk,khd->hqd', weights.astype(jnp.bfloat16), values, preferre...  12.6 us
    reduce_sum x2, other arithmetic, absorb(): total = old_total * factor + jnp.sum(weights, axis=2)  12 us
  transfers between devices with their start and end apart: 6, of which 6 were waited for; matrix products, arithmetic and copies ran while one was open for 12% of the time, Pallas kernels for 0%

commit v1 on v0

--- a/solution.py
+++ b/solution.py
@@ -110,7 +110,9 @@
         [new_keys.reshape(local_rows, -1), new_values.reshape(local_rows, -1)], axis=1
     )
     head_query = query.transpose(1, 0, 2)
-    piece = lax.all_gather(prompt_cache, "seq", axis=0, tiled=True)
+    piece = jnp.concatenate(
+        lax.all_to_all(jnp.stack([prompt_cache] * lax.axis_size("seq")), "seq", 0, 0), axis=0
+    )
     length = piece.shape[0]
     allowed = (jnp.arange(length, dtype=jnp.int32) < prompt_length)[None, :]
     split = piece.reshape(length, 2, heads_here, HD)

time: 379 us -> 498 us (1.31)
  the two profiles are of different devices: /device:TPU:12 before, /device:TPU:22 now
where the time goes in v1:
time: 498 us; the launch traced here: 497 us
  waiting for transfers between devices  343 us (69%)
  local copies, waits for them, and re-layouts  54.5 us (11%)
  matrix products  30.5 us (6%)
  other arithmetic  27.8 us (6%)
  starting transfers between devices  25.2 us (5%)
  between operations  15.9 us (3%)
    all_gather x1, waiting for transfers between devices, local(): whole = lax.all_gather(hidden_in, 'tp', axis=1, tiled=True)  197 us
    ppermute x3, waiting for transfers between devices, swapped(): return lax.ppermute(value, axis, pairs)  92.9 us
    reduce_scatter x1, waiting for transfers between devices, local(): lax.psum_scatter(lax.dot_general(w_out, attended, (((0,), (1,)), ((), ())...  52.6 us
    all_to_all x1, starting transfers between devices, local(): lax.all_to_all(jnp.stack([prompt_cache] * lax.axis_size('seq')), 'seq', 0...  19.2 us
    unnamed x49, local copies, waits for them, and re-layouts  18.1 us
    another operation x1, local copies, waits for them, and re-layouts, local(): split = piece.reshape(length, 2, heads_here, HD)  13.3 us
    dot_general x3, matrix products, absorb(): jnp.einsum('hqd,khd->hqk', queries, keys, preferred_element_type=jnp.floa...  13 us
    dot_general x3, matrix products, absorb(): jnp.einsum('hqk,khd->hqd', weights.astype(jnp.bfloat16), values, preferre...  12.6 us
  transfers between devices with their start and end apart: 6, of which 5 were waited for; matrix products, arithmetic and copies ran while one was open for 8% of the time, Pallas kernels for 0%

profile of v1, /device:TPU:22, one launch (start us, length us, event | category | flops | bytes accessed | tf_op | source)
XLA Modules:
  0.0 496.9 jit_solution(15081072633934950834)
XLA Ops:
  7.2 1.1 copy.50
  8.3 5.3 %stack.4 = bf16[64,128,2,256]{1,3,2,0:T(8,128)(2,1)} broadcast(bf16[128,2,256]{0,2,1:T(8,128)(2,1)S(1)} %copy.50), dimensions={1,2,3} | broadcast | bytes 8519680 | tf_op jit(solution)/shard_map/stack | solution.py:114
  13.6 19.2 %all-to-all-start = ((bf16[64,128,2,256]{1,3,2,0:T(8,128)(2,1)}), bf16[64,128,2,256]{1,3,2,0:T(8,128)(2,1)}, u32[]{:S(2)}, u32[]{:S(2)}) async-start(bf16[64,128,2,256]{1,3,2,0:T(8,128)(2,1)} %stack.4), calls=%async_computation | async-start | bytes 16777216 | tf_op jit(solution)/shard_map/all_to_all | solution.py:114
  32.8 0.7 all-gather.2.cloned.1.call-update
  34.5 2.0 copy.72
  36.5 2.5 copy.54
  39.0 0.6 dynamic_slice.8
  40.2 0.5 multiply_cosine_fusion
  40.8 196.8 %all-gather.2.cloned.1.call-done = bf16[256,2048]{1,0:T(8,128)(2,1)} async-done(((bf16[256,256]{1,0:T(8,128)(2,1)}), bf16[256,2048]{1,0:T(8,128)(2,1)}) %all-gather.2.cloned.1.call-update) | async-done | bytes 1048592 | tf_op jit(solution)/shard_map/all_gather | solution.py:96
  237.6 1.6 convert_reduce_fusion
  239.2 1.6 fusion.16
  240.9 2.7 fusion.62
  243.7 0.7 fusion.85
  244.8 0.9 subtract_convert_fusion.1
  246.0 1.9 collective-permute-start
  247.9 27.7 %collective-permute-done = bf16[512,2,256]{0,2,1:T(8,128)(2,1)S(1)} collective-permute-done((bf16[512,2,256]{0,2,1:T(8,128)(2,1)S(1)}, bf16[512,2,256]{0,2,1:T(8,128)(2,1)S(1)}, u32[]{:S(2)}, u32[]{:S(2)}) %collective-permute-start) | collective-permute-done | bytes 524320 | tf_op jit(solution)/shard_map/ppermute | solution.py:14
  275.7 0.3 maximum_select_fusion.2
  276.0 1.9 collective-permute-start.1
  278.0 22.1 %collective-permute-done.1 = bf16[1024,2,256]{0,2,1:T(8,128)(2,1)} collective-permute-done((bf16[1024,2,256]{0,2,1:T(8,128)(2,1)S(1)}, bf16[1024,2,256]{0,2,1:T(8,128)(2,1)}, u32[]{:S(2)}, u32[]{:S(2)}) %collective-permute-start.1) | collective-permute-done | bytes 1048608 | tf_op jit(solution)/shard_map/ppermute | solution.py:14
  300.0 3.0 maximum_select_fusion.1
  303.0 2.1 collective-permute-start.2
  305.2 0.7 dynamic-slice_bitcast_fusion
  306.1 0.7 fusion.65
  306.8 1.2 iota_compare_fusion
  308.0 43.1 %collective-permute-done.2 = bf16[2048,2,256]{0,2,1:T(8,128)(2,1)} collective-permute-done((bf16[2048,2,256]{0,2,1:T(8,128)(2,1)S(1)}, bf16[2048,2,256]{0,2,1:T(8,128)(2,1)}, u32[]{:S(2)}, u32[]{:S(2)}) %collective-permute-start.2) | collective-permute-done | bytes 2097184 | tf_op jit(solution)/shard_map/ppermute | solution.py:14
  351.0 3.8 maximum_select_fusion
  354.8 2.2 copy.73
  357.1 1.6 fusion.87
  358.7 4.5 copy.71
  363.2 2.9 copy.70
  366.2 2.2 fusion.7
  368.4 1.2 fusion.8
  369.6 0.8 copy-done.1
  370.4 1.3 copy-done.4
  371.7 2.2 fusion.9
  373.9 12.0 %copy.51 = bf16[64,128,2,256]{1,0,3,2:T(8,128)(2,1)} copy(bf16[64,128,2,256]{1,3,2,0:T(8,128)(2,1)} %all-to-all-done) | data formatting | bytes 16777216 | tf_op jit(solution)/shard_map/all_to_all | solution.py:114
  385.9 13.3 %reshape_reshape.3 = bf16[8192,2,2,128]{0,3,2,1:T(8,128)(2,1)} reshape(bf16[64,128,2,256]{1,0,3,2:T(8,128)(2,1)} %copy.51) | data formatting | bytes 16777216 | tf_op jit(solution)/shard_map/reshape;reshape | solution.py:118
  399.2 9.6 %fusion = (f32[2,256]{1,0:T(2,128)S(1)}, f32[2,256,8192]{2,1,0:T(8,128)}) fusion(pred[8192]{0:T(1024)(128)(4,1)S(1)} %iota_compare_fusion.1, bf16[8192,2,2,128]{0,3,2,1:T(8,128)(2,1)} %reshape_reshape.3, bf16[256,2,64]{2,0,1:T(8,128)(2,1)S(1)} %copy-done.13, bf16[256,2,64]{2,0,1:T(8,128)(2,1)S(1)} %copy-done.12), kind=kOutput, calls=%fused_computation.2 | convolution fusion | flops 1086586368 | bytes 21112832 | tf_op jit(solution)/shard_map/hqd,khd->hqk/dot_general | solution.py:47
  408.8 9.9 %fusion.1 = f32[2,256]{1,0:T(2,128)S(1)} fusion(f32[2,256,8192]{2,1,0:T(8,128)} %get-tuple-element.33, f32[2,256]{1,0:T(2,128)S(1)} %broadcast_maximum_fusion.1, pred[8192]{0:T(1024)(128)(4,1)S(1)} %iota_compare_fusion.1), kind=kLoop, calls=%fused_computation.3 | loop fusion | flops 16776704 | bytes 16789504 | tf_op jit(solution)/shard_map/reduce_sum | solution.py:55
  418.8 3.5 fusion.51
  422.4 0.5 copy-done.9
  422.9 1.3 fusion.45
  424.2 1.4 slice-done.1
  425.6 7.8 %fusion.57 = bf16[256,2,128]{0,2,1:T(8,128)(2,1)S(1)} fusion(f32[256,2,128]{0,2,1:T(8,128)S(1)} %fusion.45, bf16[8192,2,2,128]{0,3,2,1:T(8,128)(2,1)S(1)} %bitcast.189, f32[2,256,8192]{2,1,0:T(8,128)} %get-tuple-element.33, f32[2,256]{1,0:T(2,128)S(1)} %broadcast_maximum_fusion.1, pred[8192]{0:T(1024)(128)(4,1)S(1)} %iota_compare_fusion.1, ...), kind=kOutput, calls=%fused_computation.46 | convolution fusion | flops 1090846720 | bytes 21381120 | tf_op jit(solution)/shard_map/hqk,khd->hqd/dot_general | solution.py:56
  433.5 1.4 fusion.15
  435.0 0.9 copy.61
  435.8 52.6 %reduce-scatter.2.cloned.1.call-done = bf16[256,256]{0,1:T(8,128)(2,1)} async-done(((bf16[2048,256]{0,1:T(8,128)(2,1)}), bf16[256,256]{0,1:T(8,128)(2,1)}) %reduce-scatter.2.cloned.1.call-update) | async-done | bytes 131088 | tf_op jit(solution)/shard_map/reduce_scatter | solution.py:164
  488.4 1.6 fusion.64
  (64 shorter events, 1.3 us)
Async XLA Ops:
  7.2 426.3 %copy-start = (bf16[256,2048]{1,0:T(8,128)(2,1)S(1)}, bf16[256,2048]{1,0:T(8,128)(2,1)}, u32[]{:S(2)}) copy-start(bf16[256,2048]{1,0:T(8,128)(2,1)} %param.12) | copy-start | bytes 3145732
  13.6 20.6 %copy-start.15 = (bf16[2,128,2,256]{3,2,1,0:T(2,128)(2,1)S(1)}, bf16[2,128,2,256]{3,2,1,0:T(2,128)(2,1)}, u32[]{:S(2)}) copy-start(bf16[2,128,2,256]{3,2,1,0:T(2,128)(2,1)} %param.14) | copy-start | bytes 786436
  13.6 360.3 %all-to-all-start = ((bf16[64,128,2,256]{1,3,2,0:T(8,128)(2,1)}), bf16[64,128,2,256]{1,3,2,0:T(8,128)(2,1)}, u32[]{:S(2)}, u32[]{:S(2)}) async-start(bf16[64,128,2,256]{1,3,2,0:T(8,128)(2,1)} %stack.4), calls=%async_computation | async-start | bytes 16777216 | tf_op jit(solution)/shard_map/all_to_all | solution.py:114
  32.8 204.8 %all-gather.2.cloned.1.call-start = ((), (), s32[]{:S(2)}) async-start(), calls=%async_computation.2 | async-start | bytes 1179648 | tf_op jit(solution)/shard_map/all_gather | solution.py:96
  33.5 454.9 %reduce-scatter.2.cloned.1.call-start = ((), (), s32[]{:S(2)}) async-start(), calls=%async_computation.3 | async-start | bytes 1179648 | tf_op jit(solution)/shard_map/reduce_scatter | solution.py:164
  34.4 4.5 copy-start.17
  237.6 6.1 %copy-start.6 = (bf16[256,2048]{1,0:T(8,128)(2,1)S(1)}, bf16[256,2048]{1,0:T(8,128)(2,1)}, u32[]{:S(2)}) copy-start(bf16[256,2048]{1,0:T(8,128)(2,1)} %all-gather.2.cloned.1.call-done) | copy-start | bytes 3145732
  237.6 6.1 %copy-start.16 = (bf16[2048,256]{1,0:T(8,128)(2,1)S(1)}, bf16[2048,256]{1,0:T(8,128)(2,1)}, u32[]{:S(2)}) copy-start(bf16[2048,256]{1,0:T(8,128)(2,1)} %param.10) | copy-start | bytes 3145732
  245.9 32.0 %copy-start.10 = (bf16[256,2,128]{0,2,1:T(8,128)(2,1)}, bf16[256,2,128]{0,2,1:T(8,128)(2,1)S(1)}, u32[]{:S(2)}) copy-start(bf16[256,2,128]{0,2,1:T(8,128)(2,1)S(1)} %copy.56) | copy-start | bytes 393220
  246.0 29.7 %collective-permute-start = (bf16[512,2,256]{0,2,1:T(8,128)(2,1)S(1)}, bf16[512,2,256]{0,2,1:T(8,128)(2,1)S(1)}, u32[]{:S(2)}, u32[]{:S(2)}) collective-permute-start(bf16[512,2,256]{0,2,1:T(8,128)(2,1)S(1)} %maximum_maximum_fusion), channel_id=1, source_target_pairs={{0,8},{8,0},{16,24},{24,16},{32,40},{40,32},{48,56},{56,48},{64,72... | collective-permute-start | bytes 1572872 | tf_op jit(solution)/shard_map/ppermute | solution.py:14
  276.0 2.0 copy-start.3
  276.0 24.0 %collective-permute-start.1 = (bf16[1024,2,256]{0,2,1:T(8,128)(2,1)S(1)}, bf16[1024,2,256]{0,2,1:T(8,128)(2,1)}, u32[]{:S(2)}, u32[]{:S(2)}) collective-permute-start(bf16[1024,2,256]{0,2,1:T(8,128)(2,1)S(1)} %maximum_select_fusion.2), channel_id=1, source_target_pairs={{0,16},{8,24},{16,0},{24,8},{32,48},{40,56},{48,32},{56,40},{64,80... | collective-permute-start | bytes 3145736 | tf_op jit(solution)/shard_map/ppermute | solution.py:14
  303.0 48.0 %collective-permute-start.2 = (bf16[2048,2,256]{0,2,1:T(8,128)(2,1)S(1)}, bf16[2048,2,256]{0,2,1:T(8,128)(2,1)}, u32[]{:S(2)}, u32[]{:S(2)}) collective-permute-start(bf16[2048,2,256]{0,2,1:T(8,128)(2,1)S(1)} %maximum_select_fusion.1), channel_id=1, source_target_pairs={{0,32},{8,40},{16,48},{24,56},{32,0},{40,8},{48,16},{56,24},{64,96... | collective-permute-start | bytes 6291464 | tf_op jit(solution)/shard_map/ppermute | solution.py:14
  358.7 7.5 %copy-start.12 = (bf16[256,2,64]{2,0,1:T(8,128)(2,1)S(1)}, bf16[256,2,64]{2,0,1:T(8,128)(2,1)}, u32[]{:S(2)}) copy-start(bf16[256,2,64]{2,0,1:T(8,128)(2,1)} %get-tuple-element.10) | copy-start | bytes 196612
  358.7 7.5 %copy-start.13 = (bf16[256,2,64]{2,0,1:T(8,128)(2,1)S(1)}, bf16[256,2,64]{2,0,1:T(8,128)(2,1)}, u32[]{:S(2)}) copy-start(bf16[256,2,64]{2,0,1:T(8,128)(2,1)} %get-tuple-element.11) | copy-start | bytes 196612
  366.2 2.2 copy-start.7
  366.2 2.3 copy-start.8
  368.4 2.0 copy-start.1
  369.6 2.0 copy-start.4
  408.8 10.0 %copy-start.2 = (bf16[8,256,2,2,128]{4,1,0,3,2:T(8,128)(2,1)S(1)}, bf16[8,256,2,2,128]{4,1,0,3,2:T(8,128)(2,1)}, u32[]{:S(2)}) copy-start(bf16[8,256,2,2,128]{4,1,0,3,2:T(8,128)(2,1)} %copy.70) | copy-start | bytes 6291460
  418.8 3.6 copy-start.5
  418.8 4.1 copy-start.9
  418.8 5.4 %slice-start = ((s8[8388608]{0:T(1024)(128)(4,1)}), s8[4194304]{0:T(1024)(128)(4,1)S(1)}, s32[]{:S(2)}) async-start(s8[8388608]{0:T(1024)(128)(4,1)} %bitcast.188), calls=%async_computation.4 | async-start | bytes 8388608
  422.9 2.7 slice-start.1
  425.6 9.3 %copy-start.11 = (bf16[256,2,128]{0,2,1:T(8,128)(2,1)S(1)}, bf16[256,2,128]{0,2,1:T(8,128)(2,1)}, u32[]{:S(2)}) copy-start(bf16[256,2,128]{0,2,1:T(8,128)(2,1)} %copy-done.10) | copy-start | bytes 393220
  433.4 55.0 %copy-start.14 = (bf16[256,256]{1,0:T(8,128)(2,1)S(1)}, bf16[256,256]{1,0:T(8,128)(2,1)}, u32[]{:S(2)}) copy-start(bf16[256,256]{1,0:T(8,128)(2,1)} %param.9) | copy-start | bytes 393220
Sparse Core Ops, SparseCore 0:
  35.6 201.9 all-gather.1
  435.0 53.3 reduce-scatter.1
